TPU v7x, 256 devices: a whole 4x4x8 slice. The times are simulated.
256 devices in a mesh: ta: 32 (over z, y_lo, core), ka: 8 (over y_hi, x).
Axes of the slice: x: 4, y: 4 (y_hi: 2, y_lo: 2; y = y_hi * 2 + y_lo), z: 8, core: 2. Of those that a mesh axis runs over, the one named last changes fastest.
Arguments:
- green_row: float32 [2, 4, 4, 64, 1024], P(None, None, None, 'ta', 'ka'), may hold values from -6 to 6
- screen_lesser: float32 [2, 4, 4, 64, 1024], P(None, None, None, 'ta', 'ka'), may hold values from -6 to 6
- screen_retarded: float32 [2, 4, 4, 64, 1024], P(None, None, None, 'ta', 'ka'), may hold values from -6 to 6
- onsite: float32 [2, 4, 4], replicated, may hold values from -3 to 3
- lesser_slab: bfloat16 [2, 4, 4, 64, 64, 1024], P(None, None, None, 'ta', None, 'ka'), may hold values from -0.5 to 0.5
- advanced_slab: bfloat16 [2, 4, 4, 64, 64, 1024], P(None, None, None, 'ta', None, 'ka'), may hold values from -0.5 to 0.5
- slab_start: int32 [1], replicated, may hold values from 0 to 4095
- block_table: int32 [32], replicated, may hold values from 0 to 31, each once
Outputs:
- next_row: float32 [2, 4, 4, 64, 1024], P(None, None, None, 'ta', 'ka')
- derivative: float32 [2, 4, 4, 64, 1024], P(None, None, None, 'ta', 'ka')
Inputs may be any that keep to these rules, and one draw needn't show every extreme that they name: block_table is a permutation: each time block 0 to 31 appears once.
All inputs are finite; a program needn't handle non-finite values.
Results may differ from a plain program's by a relative error of at most 0.0019.
Values sent between devices are 32-bit elements; how exact they have to be, the bound alone decides.
A program may use at most 64 MiB of HBM per device.

v0:
```python
import math

import jax
import jax.numpy as jnp
import numpy as np
from jax import lax
from jax.experimental import pallas as pl
from jax.experimental.pallas import tpu as pltpu
from jax.sharding import PartitionSpec as P

KS = 32
MESH = pl.DeviceIdType.MESH
F32 = jnp.float32
BF16 = jnp.bfloat16

time_step = 0.1
drive_amp = 1.0
drive_freq = 0.37


def split_np(x):
    hi = x.astype(np.float32).astype(jnp.bfloat16)
    lo = (x - hi.astype(np.float64)).astype(np.float32).astype(jnp.bfloat16)
    return hi, lo


def tables():
    ka, x1 = np.meshgrid(np.arange(8), np.arange(8), indexing="ij")
    c8, s8 = np.cos(2 * np.pi * ka * x1 / 8), np.sin(2 * np.pi * ka * x1 / 8)
    eye = np.eye(4)
    fwd = np.zeros((2, 8, 4, 8, 2, 4))
    bwd = np.zeros((8, 2, 4, 2, 8, 4))
    for k in range(8):
        for x in range(8):
            c, s = c8[k, x] * eye / KS, s8[k, x] * eye / KS
            fwd[0, x, :, k, 0, :] = c
            fwd[0, x, :, k, 1, :] = -s
            fwd[1, x, :, k, 0, :] = s
            fwd[1, x, :, k, 1, :] = c
            bwd[k, 0, :, 0, x, :] = c
            bwd[k, 0, :, 1, x, :] = s
            bwd[k, 1, :, 0, x, :] = -s
            bwd[k, 1, :, 1, x, :] = c
    left = []
    for m in (fwd.reshape(64, 64), bwd.reshape(64, 64)):
        hi, lo = split_np(m)
        left.append(np.concatenate([hi, lo, hi], axis=1))
    left = np.stack(left)
    lane = np.arange(128)
    j, y = lane // 32, lane % 32
    angle = 2 * np.pi * (np.outer(j, j) / 4 + np.outer(y, y) / 32)
    c, s = np.cos(angle), np.sin(angle)
    right = []
    for m in (np.block([[c, s], [-s, c]]), np.block([[c, -s], [s, c]])):
        right.extend(split_np(m))
    right = np.stack(right)
    row = np.arange(32) // 4
    tw = 2 * np.pi * np.outer(row, j) / 32
    twiddle = np.stack([np.cos(tw), np.sin(tw)]).astype(np.float32)
    return left, right, twiddle


def split(x):
    hi = x.astype(BF16)
    lo = (x - hi.astype(F32)).astype(BF16)
    return hi, lo


def mm(a, b):
    return jnp.dot(a, b, preferred_element_type=F32)


def left_product(table, x):
    hi, lo = split(x)
    return mm(table, jnp.concatenate([hi, hi, lo], axis=0))


def right_product(hi_table, lo_table, x):
    rows = x.shape[0]
    hi, lo = split(x)
    both = mm(jnp.concatenate([hi, lo], axis=0), hi_table)
    return both[:rows] + both[rows:] + mm(hi, lo_table)


def order(i):
    half = (i + 1) // 2
    return 4 + half - 2 * half * (i % 2)


def kernel(
    onsite, table, green, less, ret, energy, adv_hbm, les_hbm, left, right, twiddle,
    next_row, derivative,
    raw, slab, isend, irecv, gsend, grecv, screens, ssend, srecv, sig,
    out_o, cown, crecv, ysend, yrecv, zsend, zrecv,
    gbuf, hg, first,
    raw_sem, is_sem, ir_sem, gs_sem, gr_sem, ss_sem, sr_sem,
    cs_sem, cr_sem, ys_sem, yr_sem, zs_sem, zr_sem,
):
    ta, ka = lax.axis_index("ta"), lax.axis_index("ka")
    z, y, core = ta // 4, (ta // 2) % 2, ta % 2
    sibling = ta + 1 - 2 * core
    across = ta + 2 - 4 * y

    adv_copy = pltpu.make_async_copy(adv_hbm, raw.at[0], raw_sem.at[0])
    les_copy = pltpu.make_async_copy(les_hbm, raw.at[1], raw_sem.at[1])
    adv_copy.start()
    les_copy.start()

    barrier = pltpu.get_barrier_semaphore()
    for i in range(1, 8):
        pl.semaphore_signal(barrier, inc=1, device_id=(ta, (ka + i) % 8), device_id_type=MESH)
        pl.semaphore_signal(barrier, inc=1, device_id=((ta + 4 * i) % 32, ka), device_id_type=MESH)
    pl.semaphore_signal(barrier, inc=1, device_id=(sibling, ka), device_id_type=MESH)
    pl.semaphore_signal(barrier, inc=1, device_id=(across, ka), device_id_type=MESH)

    for n, ref in enumerate((less, ret, green)):
        for d in range(8):
            isend[d, 8 * n : 8 * n + 8, :] = ref[pl.ds(d, 8, stride=8), :]
    gbuf[...] = green[...]
    pl.semaphore_wait(barrier, 16)

    sends = []

    def push(src, dst, ssem, rsem, to):
        copy = pltpu.make_async_remote_copy(
            src_ref=src, dst_ref=dst, send_sem=ssem, recv_sem=rsem,
            device_id=to, device_id_type=MESH,
        )
        copy.start()
        return copy

    def arrived(dst, rsem):
        pltpu.make_async_remote_copy(
            src_ref=dst, dst_ref=dst, send_sem=rsem, recv_sem=rsem,
            device_id=(ta, ka), device_id_type=MESH,
        ).wait_recv()

    def exchange(src, dst, ssem, rsem):
        for i in range(1, 8):
            peer = (ka + i) % 8
            sends.append(push(src.at[peer], dst.at[ka], ssem.at[i], rsem.at[ka], (ta, peer)))
        dst[ka] = src[ka]

    def collect(dst, rsem):
        for i in range(1, 8):
            peer = (ka + i) % 8
            arrived(dst.at[peer], rsem.at[peer])

    exchange(isend, irecv, is_sem, ir_sem)

    row = lax.broadcasted_iota(jnp.int32, (256, 256), 0)
    col = lax.broadcasted_iota(jnp.int32, (256, 256), 1)
    place = row // 8
    source = (
        ((row // 2) % 4) * 64 + (place % 8) * 8 + ((place // 8) % 2) * 4 + (place // 16) * 2 + row % 2
    )
    picked = source == col
    lane = lax.broadcasted_iota(jnp.int32, (1, 256), 1) % 64
    tau = jnp.zeros((1, 256), jnp.int32)
    for i in range(32):
        tau = jnp.where(lane // 2 == i, 2 * table[i], tau)
    tau = tau + lane % 2
    own = 2 * table[ta]
    plain = jnp.where(picked, 1.0, 0.0).astype(BF16)
    masked = [
        jnp.where(picked & (own + s <= tau), 1.0, 0.0).astype(BF16) for s in range(2)
    ]
    adv_copy.wait()
    les_copy.wait()

    def relay(b, carry):
        for kind in range(2):
            for s in range(2):
                parts = [
                    jnp.concatenate([raw[kind, q, b, c, s] for c in range(4)], axis=0)
                    for q in range(2)
                ]
                moved = mm(masked[s] if kind == 0 else plain, jnp.concatenate(parts, axis=1))
                re, im = moved[:, :128], moved[:, 128:]
                d = b * 2 + s
                slab[kind, 0, d] = re.reshape(32, 8, 128)
                slab[kind, 1, d] = im.reshape(32, 8, 128)
                slab[kind, 2, d] = (re + im).reshape(32, 8, 128)
        return carry

    lax.fori_loop(0, 4, relay, 0)

    tw_c, tw_s = twiddle[0], twiddle[1]

    def to_space(tiles):
        mixed = left_product(left[0], tiles)
        n = tiles.shape[1] // 128
        turned = []
        for i in range(n):
            re, im = (mixed[32 * p : 32 * p + 32, 128 * i : 128 * i + 128] for p in range(2))
            turned.append(
                jnp.concatenate([re * tw_c - im * tw_s, re * tw_s + im * tw_c], axis=1)
            )
        out = right_product(right[0], right[1], jnp.concatenate(turned, axis=0))
        return [out[32 * i : 32 * i + 32] for i in range(n)]

    def to_momenta(fields):
        out = right_product(right[2], right[3], jnp.concatenate(fields, axis=0))
        turned = []
        for i in range(2):
            re, im = out[32 * i : 32 * i + 32, :128], out[32 * i : 32 * i + 32, 128:]
            turned.append(
                jnp.concatenate([re * tw_c + im * tw_s, im * tw_c - re * tw_s], axis=0)
            )
        return left_product(left[1], jnp.concatenate(turned, axis=1))

    collect(irecv, ir_sem)
    tiles = jnp.concatenate(
        [irecv[:, 8 * n : 8 * n + 8, :].reshape(64, 128) for n in range(3)], axis=1
    )
    w_less, w_ret, space = to_space(tiles)
    screens[0] = w_less
    screens[1] = w_ret

    def blocks(group, i0):
        js = [group * 8 + (z + order(i0 + n)) % 8 for n in range(2)]
        acc = [[[None] * 3 for _ in range(4)] for _ in range(2)]
        for kind in range(2):
            for d in range(8):
                for q in range(3):
                    values = [slab[kind, q, d, js[n]] for n in range(2)]
                    for a in range(4):
                        factor = sig[kind, q, d, a]
                        for n in range(2):
                            term = factor * values[n]
                            old = acc[n][a][q]
                            acc[n][a][q] = term if old is None else old + term
        out = []
        for n in range(2):
            re = [acc[n][a][0] - acc[n][a][1] for a in range(4)]
            im = [acc[n][a][2] - acc[n][a][0] - acc[n][a][1] for a in range(4)]
            out.append(re + im)
        return out

    def reduced(r):
        def for_sibling(half, group):
            def body(piece, carry):
                out = blocks(group, 2 * piece)
                for n in range(2):
                    for m in range(8):
                        out_o[r, half, 2 * piece + n, m] = out[n][m]
                push(
                    out_o.at[r, half, pl.ds(2 * piece, 2)], crecv.at[r, half, pl.ds(2 * piece, 2)],
                    cs_sem.at[r, half, piece], cr_sem.at[r, half, piece], (sibling, ka),
                )
                return carry

            lax.fori_loop(0, 4, body, 0)

        def from_sibling(half, piece):
            arrived(crecv.at[r, half, pl.ds(2 * piece, 2)], cr_sem.at[r, half, piece])

        for_sibling(0, (1 - core) * 2 + 1 - y)

        def to_across(piece, carry):
            out = blocks(core * 2 + 1 - y, 2 * piece)
            from_sibling(0, piece)
            for n in range(2):
                for m in range(8):
                    ysend[r, 2 * piece + n, m] = out[n][m] + crecv[r, 0, 2 * piece + n, m]
            push(
                ysend.at[r, pl.ds(2 * piece, 2)], yrecv.at[r, pl.ds(2 * piece, 2)],
                ys_sem.at[r, piece], yr_sem.at[r, piece], (across, ka),
            )
            return carry

        lax.fori_loop(0, 4, to_across, 0)
        for_sibling(1, (1 - core) * 2 + y)

        def mine(piece, carry):
            out = blocks(core * 2 + y, 2 * piece)
            from_sibling(1, piece)
            for n in range(2):
                for m in range(8):
                    cown[2 * piece + n, m] = out[n][m] + crecv[r, 1, 2 * piece + n, m]
            return carry

        lax.fori_loop(0, 4, mine, 0)

        for i in range(8):
            if i % 2 == 0:
                arrived(yrecv.at[r, pl.ds(i, 2)], yr_sem.at[r, i // 2])
            zsend[r, i] = cown[i] + yrecv[r, i]
            if i < 7:
                away = (z + order(i)) % 8
                sends.append(
                    push(
                        zsend.at[r, i], zrecv.at[r, z], zs_sem.at[r, i], zr_sem.at[r, z],
                        (away * 4 + ta % 4, ka),
                    )
                )
        total = zsend[r, 7]
        for i in range(1, 8):
            peer = (z + i) % 8
            arrived(zrecv.at[r, peer], zr_sem.at[r, peer])
            total = total + zrecv[r, peer]
        for half in range(2):
            for piece in range(4):
                pltpu.make_async_remote_copy(
                    src_ref=out_o.at[r, half, pl.ds(2 * piece, 2)],
                    dst_ref=crecv.at[r, half, pl.ds(2 * piece, 2)],
                    send_sem=cs_sem.at[r, half, piece], recv_sem=cr_sem.at[r, half, piece],
                    device_id=(sibling, ka), device_id_type=MESH,
                ).wait_send()
        for piece in range(4):
            pltpu.make_async_remote_copy(
                src_ref=ysend.at[r, pl.ds(2 * piece, 2)], dst_ref=yrecv.at[r, pl.ds(2 * piece, 2)],
                send_sem=ys_sem.at[r, piece], recv_sem=yr_sem.at[r, piece],
                device_id=(across, ka), device_id_type=MESH,
            ).wait_send()
        return total

    for r in range(3):
        if r > 0:
            for d in range(8):
                gsend[r - 1, d] = gbuf[pl.ds(d, 8, stride=8), :]
            exchange(gsend.at[r - 1], grecv.at[r - 1], gs_sem.at[r - 1], gr_sem.at[r - 1])
            collect(grecv.at[r - 1], gr_sem.at[r - 1])
            (space,) = to_space(grecv[r - 1].reshape(64, 128))
        re, im = space[:, :128], space[:, 128:]
        fields = []
        for kind in range(2):
            w_re, w_im = screens[kind, :, :128], screens[kind, :, 128:]
            fields.append(
                jnp.concatenate([-(re * w_im + im * w_re), re * w_re - im * w_im], axis=1)
            )
        sigma = to_momenta(fields)
        for kind in range(2):
            ssend[r, :, kind] = sigma[:, 128 * kind : 128 * kind + 128].reshape(8, 8, 128)
        exchange(ssend.at[r], srecv.at[r], ss_sem.at[r], sr_sem.at[r])

        e = energy[...]
        rows = [gbuf[8 * m : 8 * m + 8] for m in range(8)]
        for a in range(4):
            re, im = e * rows[a], e * rows[4 + a]
            for b in range(4):
                o_re, o_im = onsite[4 * a + b], onsite[16 + 4 * a + b]
                re = re + o_re * rows[b] - o_im * rows[4 + b]
                im = im + o_re * rows[4 + b] + o_im * rows[b]
            hg[a] = re
            hg[4 + a] = im

        collect(srecv.at[r], sr_sem.at[r])
        for kind in range(2):
            for d in range(8):
                tile = srecv[r, d, kind].astype(BF16).astype(F32)
                for a in range(4):
                    s_re = jnp.broadcast_to(tile[a : a + 1], (8, 128))
                    s_im = jnp.broadcast_to(tile[4 + a : 5 + a], (8, 128))
                    sig[kind, 0, d, a] = s_re
                    sig[kind, 1, d, a] = s_im
                    sig[kind, 2, d, a] = s_re + s_im

        total = reduced(r) + hg[...]
        rate = jnp.concatenate([total[4:], -total[:4]], axis=0).reshape(64, 128)
        if r == 0:
            first[...] = rate
            gbuf[...] = green[...] + time_step * rate
        elif r == 1:
            gbuf[...] = green[...] + (0.5 * time_step) * (first[...] + rate)
        else:
            next_row[...] = green[...] + (0.5 * time_step) * (first[...] + rate)
            derivative[...] = rate

    for copy in sends:
        copy.wait_send()


def dispersion(slab_start, all_times, kx_ids, ky_ids):
    current = (slab_start[0] + all_times).astype(jnp.float32)
    shift = drive_amp * jnp.sin(drive_freq * current)
    factor = 2.0 * math.pi / KS
    return -2.0 * (
        jnp.cos(kx_ids.astype(jnp.float32) * factor + shift)
        + jnp.cos(ky_ids.astype(jnp.float32) * factor)
    )


def local(
    green_row, screen_lesser, screen_retarded, onsite, lesser_slab, advanced_slab, slab_start,
    block_table,
):
    k_local = green_row.shape[4]
    ka_index = lax.axis_index("ka")
    momenta = ka_index * k_local + jnp.arange(k_local, dtype=jnp.int32)
    energy = dispersion(slab_start, 64, momenta // KS, momenta % KS).reshape(1, k_local)
    left, right, twiddle = tables()

    def vmem():
        return pl.BlockSpec(memory_space=pltpu.VMEM)

    def smem():
        return pl.BlockSpec(memory_space=pltpu.SMEM)

    def scratch(*dims, kind=F32):
        return pltpu.VMEM(dims, kind)

    def sems(*dims):
        return pltpu.SemaphoreType.DMA(dims)

    rows = jax.ShapeDtypeStruct((64, 128), F32)
    next_row, derivative = pl.pallas_call(
        kernel,
        name="gw_step",
        out_shape=(rows, rows),
        in_specs=[smem(), smem()] + [vmem()] * 4 + [pl.BlockSpec(memory_space=pl.ANY)] * 2
        + [vmem()] * 3,
        out_specs=(vmem(), vmem()),
        scratch_shapes=[
            scratch(2, 2, 4, 4, 2, 64, 128, kind=BF16),
            scratch(2, 3, 8, 32, 8, 128),
            scratch(8, 24, 128),
            scratch(8, 24, 128),
            scratch(2, 8, 8, 128),
            scratch(2, 8, 8, 128),
            scratch(2, 32, 256),
            scratch(3, 8, 2, 8, 128),
            scratch(3, 8, 2, 8, 128),
            scratch(2, 3, 8, 4, 8, 128),
            scratch(3, 2, 8, 8, 8, 128),
            scratch(8, 8, 8, 128),
            scratch(3, 2, 8, 8, 8, 128),
            scratch(3, 8, 8, 8, 128),
            scratch(3, 8, 8, 8, 128),
            scratch(3, 8, 8, 8, 128),
            scratch(3, 8, 8, 8, 128),
            scratch(64, 128),
            scratch(8, 8, 128),
            scratch(64, 128),
            sems(2),
            sems(8), sems(8),
            sems(2, 8), sems(2, 8),
            sems(3, 8), sems(3, 8),
            sems(3, 2, 4), sems(3, 2, 4),
            sems(3, 4), sems(3, 4),
            sems(3, 8), sems(3, 8),
        ],
        compiler_params=pltpu.CompilerParams(
            collective_id=0, has_side_effects=True, vmem_limit_bytes=48 * 2**20
        ),
    )(
        onsite.reshape(32),
        block_table,
        green_row.reshape(64, 128),
        screen_lesser.reshape(64, 128),
        screen_retarded.reshape(64, 128),
        energy,
        advanced_slab,
        lesser_slab,
        jnp.asarray(left),
        jnp.asarray(right),
        jnp.asarray(twiddle),
    )
    return next_row.reshape(green_row.shape), derivative.reshape(green_row.shape)


def solution(mesh):
    return jax.shard_map(
        local,
        mesh=mesh,
        in_specs=(
            P(None, None, None, "ta", "ka"),
            P(None, None, None, "ta", "ka"),
            P(None, None, None, "ta", "ka"),
            P(),
            P(None, None, None, "ta", None, "ka"),
            P(None, None, None, "ta", None, "ka"),
            P(),
            P(),
        ),
        out_specs=(P(None, None, None, "ta", "ka"), P(None, None, None, "ta", "ka")),
        check_vma=False,
    )
```

profile of v0, /device:TPU:1, one launch (start us, length us, event | category | flops | bytes accessed | tf_op | source)
XLA Modules:
  0.0 93.5 jit_solution(15272754937213326010)
XLA Ops:
  0.6 0.0 copy-start.7
  1.4 0.1 fusion.4.energy
  1.4 0.0 copy-start.8
  1.5 0.8 reshape.127.onsite
  2.2 0.0 copy-done.7
  2.2 0.0 copy-done.8
  2.2 0.0 copy-start
  2.3 1.2 %copy-done = bf16[2,4,4,2,64,128]{5,4,3,2,1,0:T(8,128)(2,1)S(1)} copy-done((bf16[2,4,4,2,64,128]{5,4,3,2,1,0:T(8,128)(2,1)S(1)}, bf16[2,4,4,2,64,128]{5,4,3,2,1,0:T(8,128)(2,1)}, u32[]{:S(2)}) %copy-start) | copy-done | bytes 1048600
  3.5 0.0 copy-start.1
  3.5 1.2 %copy-done.1 = bf16[2,4,4,2,64,128]{5,4,3,2,1,0:T(8,128)(2,1)S(1)} copy-done((bf16[2,4,4,2,64,128]{5,4,3,2,1,0:T(8,128)(2,1)S(1)}, bf16[2,4,4,2,64,128]{5,4,3,2,1,0:T(8,128)(2,1)}, u32[]{:S(2)}) %copy-start.1) | copy-done | bytes 1048600
  4.7 0.0 copy-start.2
  4.7 1.0 %copy-done.2 = bf16[4,256,256]{2,1,0:T(8,128)(2,1)S(1)} copy-done((bf16[4,256,256]{2,1,0:T(8,128)(2,1)S(1)}, bf16[4,256,256]{2,1,0:T(8,128)(2,1)}, u32[]{:S(2)}) %copy-start.2) | copy-done | bytes 524312
  5.7 0.0 copy-start.3
  5.7 0.8 copy-done.3
  6.6 0.0 copy-start.4
  6.6 0.8 copy-done.4
  7.3 0.0 copy-start.5
  7.3 0.8 copy-done.5
  8.1 0.0 copy-start.6
  8.1 0.8 copy-done.6
  8.9 83.4 %gw_step.1 = (f32[64,128]{1,0:T(8,128)S(1)}, f32[64,128]{1,0:T(8,128)S(1)}) custom-call(f32[32]{0:T(128)S(1)} %reshape.127.onsite, s32[32]{0:T(128)S(1)} %copy-done.8, f32[64,128]{1,0:T(8,128)S(1)} %bitcast.6, f32[64,128]{1,0:T(8,128)S(1)} %bitcast.7, f32[64,128]{1,0:T(8,128)S(1)} %bitcast.8, f32[1,128]{1,0:T(1,128)S(1)} %fusion.4.energy, ...), custom_call_target="tpu_custom_call" | custom-call | tf_op jit(solution)/shard_map/gw_step/pallas_call | solution.py:407
  92.2 0.6 copy.16
  92.8 0.6 copy.17
Async XLA Ops:
  0.6 1.6 %copy-start.7 = (f32[2,32,128]{2,1,0:T(8,128)S(1)}, f32[2,32,128]{2,1,0:T(8,128)}, u32[]{:S(2)}) copy-start(f32[2,32,128]{2,1,0:T(8,128)} %constant.52.clone.twiddle) | copy-start | bytes 98308
  1.4 0.8 copy-start.8
  2.2 1.2 %copy-start = (bf16[2,4,4,2,64,128]{5,4,3,2,1,0:T(8,128)(2,1)S(1)}, bf16[2,4,4,2,64,128]{5,4,3,2,1,0:T(8,128)(2,1)}, u32[]{:S(2)}) copy-start(bf16[2,4,4,2,64,128]{5,4,3,2,1,0:T(8,128)(2,1)} %adv_hbm.1) | copy-start | bytes 3145732
  3.5 1.2 %copy-start.1 = (bf16[2,4,4,2,64,128]{5,4,3,2,1,0:T(8,128)(2,1)S(1)}, bf16[2,4,4,2,64,128]{5,4,3,2,1,0:T(8,128)(2,1)}, u32[]{:S(2)}) copy-start(bf16[2,4,4,2,64,128]{5,4,3,2,1,0:T(8,128)(2,1)} %les_hbm.1) | copy-start | bytes 3145732
  4.7 1.0 %copy-start.2 = (bf16[4,256,256]{2,1,0:T(8,128)(2,1)S(1)}, bf16[4,256,256]{2,1,0:T(8,128)(2,1)}, u32[]{:S(2)}) copy-start(bf16[4,256,256]{2,1,0:T(8,128)(2,1)} %constant.51.clone.right) | copy-start | bytes 1572868
  5.7 0.8 copy-start.3
  6.6 0.8 copy-start.4
  7.3 0.8 copy-start.5
  8.1 0.8 copy-start.6
where the time goes:
time: 94 us; the launch traced here: 93.5 us
  Pallas kernels  83.4 us (89%)
  local copies, waits for them, and re-layouts  8.62 us (9%)
  between operations  1.42 us (2%)
    pallas_call x1, Pallas kernels, local(): pl.pallas_call(kernel, name='gw_step', out_shape=(rows, rows), in_specs=[...  83.4 us
    unnamed x20, local copies, waits for them, and re-layouts  7.84 us

commit v1 on v0

v1 whole, which is shorter than its diff:
```python
import math

import jax
import jax.numpy as jnp
import numpy as np
from jax import lax
from jax.experimental import pallas as pl
from jax.experimental.pallas import tpu as pltpu
from jax.sharding import PartitionSpec as P

KS = 32
MESH = pl.DeviceIdType.MESH
F32 = jnp.float32
BF16 = jnp.bfloat16

time_step = 0.1
drive_amp = 1.0
drive_freq = 0.37


def split_np(x):
    hi = x.astype(np.float32).astype(jnp.bfloat16)
    lo = (x - hi.astype(np.float64)).astype(np.float32).astype(jnp.bfloat16)
    return hi, lo


def tables():
    ka, x1 = np.meshgrid(np.arange(8), np.arange(8), indexing="ij")
    c8, s8 = np.cos(2 * np.pi * ka * x1 / 8), np.sin(2 * np.pi * ka * x1 / 8)
    eye = np.eye(4)
    fwd = np.zeros((2, 8, 4, 8, 2, 4))
    bwd = np.zeros((8, 2, 4, 2, 8, 4))
    for k in range(8):
        for x in range(8):
            c, s = c8[k, x] * eye / KS, s8[k, x] * eye / KS
            fwd[0, x, :, k, 0, :] = c
            fwd[0, x, :, k, 1, :] = -s
            fwd[1, x, :, k, 0, :] = s
            fwd[1, x, :, k, 1, :] = c
            bwd[k, 0, :, 0, x, :] = c
            bwd[k, 0, :, 1, x, :] = s
            bwd[k, 1, :, 0, x, :] = -s
            bwd[k, 1, :, 1, x, :] = c
    left = []
    for m in (fwd.reshape(64, 64), bwd.reshape(64, 64)):
        hi, lo = split_np(m)
        left.append(np.concatenate([hi, lo, hi], axis=1))
    left = np.stack(left)
    lane = np.arange(128)
    j, y = lane // 32, lane % 32
    angle = 2 * np.pi * (np.outer(j, j) / 4 + np.outer(y, y) / 32)
    c, s = np.cos(angle), np.sin(angle)
    right = []
    for m in (np.block([[c, s], [-s, c]]), np.block([[c, -s], [s, c]])):
        right.extend(split_np(m))
    right = np.stack(right)
    row = np.arange(32) // 4
    tw = 2 * np.pi * np.outer(row, j) / 32
    twiddle = np.stack([np.cos(tw), np.sin(tw)]).astype(np.float32)
    return left, right, twiddle


def split(x):
    hi = x.astype(BF16)
    lo = (x - hi.astype(F32)).astype(BF16)
    return hi, lo


def mm(a, b):
    return jnp.dot(a, b, preferred_element_type=F32)


def left_product(table, x):
    hi, lo = split(x)
    return mm(table, jnp.concatenate([hi, hi, lo], axis=0))


def right_product(hi_table, lo_table, x):
    rows = x.shape[0]
    hi, lo = split(x)
    both = mm(jnp.concatenate([hi, lo], axis=0), hi_table)
    return both[:rows] + both[rows:] + mm(hi, lo_table)


def order(i):
    half = (i + 1) // 2
    return 4 + half - 2 * half * (i % 2)


def kernel(
    onsite_hbm, table_hbm, begin_hbm, green_hbm, less_hbm, ret_hbm, adv_hbm, les_hbm,
    left_hbm, right_hbm, twiddle_hbm,
    next_row, derivative,
    onsite, table, begin, green, less, ret, left, right, twiddle,
    raw, slab, oslab, isend, irecv, gsend, grecv, screens, ssend, srecv, sig,
    own, ysend, yrecv, zsend, zrecv, gbuf, hg, first,
    in_sem, os_sem, or_sem, is_sem, ir_sem, gs_sem, gr_sem, ss_sem, sr_sem,
    ys_sem, yr_sem, zs_sem, zr_sem,
):
    ta, ka = lax.axis_index("ta"), lax.axis_index("ka")
    z, y, core = ta // 4, (ta // 2) % 2, ta % 2
    sibling = ta + 1 - 2 * core
    across = ta + 2 - 4 * y

    loads = [
        pltpu.make_async_copy(src, dst, in_sem.at[i])
        for i, (src, dst) in enumerate(
            (
                (less_hbm, less), (ret_hbm, ret), (green_hbm, green), (table_hbm, table),
                (adv_hbm, raw.at[0]), (les_hbm, raw.at[1]), (onsite_hbm, onsite),
                (begin_hbm, begin), (left_hbm, left), (right_hbm, right), (twiddle_hbm, twiddle),
            )
        )
    ]
    for copy in loads:
        copy.start()

    barrier = pltpu.get_barrier_semaphore()
    for i in range(1, 8):
        pl.semaphore_signal(barrier, inc=1, device_id=(ta, (ka + i) % 8), device_id_type=MESH)
        pl.semaphore_signal(barrier, inc=1, device_id=(sibling, (ka + i) % 8), device_id_type=MESH)
        pl.semaphore_signal(barrier, inc=1, device_id=((ta + 4 * i) % 32, ka), device_id_type=MESH)
    pl.semaphore_signal(barrier, inc=1, device_id=(sibling, ka), device_id_type=MESH)
    pl.semaphore_signal(barrier, inc=1, device_id=(across, ka), device_id_type=MESH)

    row = lax.broadcasted_iota(jnp.int32, (256, 1), 0)
    col = lax.broadcasted_iota(jnp.int32, (256, 256), 1)
    place = row // 8
    source = (
        ((row // 2) % 4) * 64 + (place % 8) * 8 + ((place // 8) % 2) * 4
        + ((core + place // 16) % 2) * 2 + row % 2
    )
    picked = source == col
    lane = lax.broadcasted_iota(jnp.int32, (1, 256), 1) % 64
    for copy in loads[:4]:
        copy.wait()
    for n, ref in enumerate((less, ret, green)):
        for d in range(8):
            isend[d, 8 * n : 8 * n + 8, :] = ref[pl.ds(d, 8, stride=8), :]
    gbuf[...] = green[...]
    tau = jnp.zeros((1, 256), jnp.int32)
    for i in range(32):
        tau = jnp.where(lane // 2 == i, 2 * table[i], tau)
    tau = tau + lane % 2
    now = 2 * table[ta]
    plain = jnp.where(picked, 1.0, 0.0).astype(BF16)
    masked = [
        jnp.where(picked & (now + s <= tau), 1.0, 0.0).astype(BF16) for s in range(2)
    ]
    for copy in loads[4:]:
        copy.wait()

    def relay(b, carry):
        for kind in range(2):
            for s in range(2):
                parts = [
                    jnp.concatenate([raw[kind, q, b, c, s] for c in range(4)], axis=0)
                    for q in range(2)
                ]
                moved = mm(masked[s] if kind == 0 else plain, jnp.concatenate(parts, axis=1))
                re, im = moved[:, :128], moved[:, 128:]
                d = b * 2 + s
                slab[kind, 0, core * 8 + d] = re[:128].reshape(16, 8, 128)
                slab[kind, 1, core * 8 + d] = im[:128].reshape(16, 8, 128)
                slab[kind, 2, core * 8 + d] = (re[:128] + im[:128]).reshape(16, 8, 128)
                oslab[kind, 0, d] = re[128:].reshape(16, 8, 128)
                oslab[kind, 1, d] = im[128:].reshape(16, 8, 128)
        return carry

    lax.fori_loop(0, 4, relay, 0)

    pl.semaphore_wait(barrier, 23)

    def describe(src, dst, ssem, rsem, to):
        return pltpu.make_async_remote_copy(
            src_ref=src, dst_ref=dst, send_sem=ssem, recv_sem=rsem,
            device_id=to, device_id_type=MESH,
        )

    def push(src, dst, ssem, rsem, to):
        describe(src, dst, ssem, rsem, to).start()

    def arrived(dst, rsem):
        describe(dst, dst, rsem, rsem, (sibling, ka)).wait_recv()

    def sent(src, ssem):
        describe(src, src, ssem, ssem, (sibling, ka)).wait_send()

    def exchange(src, dst, ssem, rsem):
        for i in range(7, 0, -1):
            peer = (ka + i) % 8
            push(src.at[peer], dst.at[ka], ssem.at[i], rsem.at[ka], (ta, peer))
        dst[ka] = src[ka]

    def collect(dst, rsem):
        for i in range(1, 8):
            peer = (ka + i) % 8
            arrived(dst.at[peer], rsem.at[peer])

    exchange(isend, irecv, is_sem, ir_sem)
    for kind in range(2):
        for q in range(2):
            push(
                oslab.at[kind, q], slab.at[kind, q, pl.ds(core * 8, 8)],
                os_sem.at[kind, q], or_sem.at[kind, q], (sibling, ka),
            )

    shift = drive_amp * jnp.sin(
        jnp.full((8, 128), drive_freq, F32) * (begin[0] + 64).astype(F32)
    )
    k_lane = lax.broadcasted_iota(jnp.int32, (8, 128), 1)
    factor = 2.0 * math.pi / KS
    e = -2.0 * (
        jnp.cos((4 * ka + k_lane // KS).astype(F32) * factor + shift)
        + jnp.cos((k_lane % KS).astype(F32) * factor)
    )

    tw_c, tw_s = twiddle[0], twiddle[1]

    def to_space(tiles):
        mixed = left_product(left[0], tiles)
        n = tiles.shape[1] // 128
        turned = []
        for i in range(n):
            re, im = (mixed[32 * p : 32 * p + 32, 128 * i : 128 * i + 128] for p in range(2))
            turned.append(
                jnp.concatenate([re * tw_c - im * tw_s, re * tw_s + im * tw_c], axis=1)
            )
        out = right_product(right[0], right[1], jnp.concatenate(turned, axis=0))
        return [out[32 * i : 32 * i + 32] for i in range(n)]

    def to_momenta(fields):
        out = right_product(right[2], right[3], jnp.concatenate(fields, axis=0))
        turned = []
        for i in range(2):
            re, im = out[32 * i : 32 * i + 32, :128], out[32 * i : 32 * i + 32, 128:]
            turned.append(
                jnp.concatenate([re * tw_c + im * tw_s, im * tw_c - re * tw_s], axis=0)
            )
        return left_product(left[1], jnp.concatenate(turned, axis=1))

    collect(irecv, ir_sem)
    tiles = jnp.concatenate(
        [irecv[:, 8 * n : 8 * n + 8, :].reshape(64, 128) for n in range(3)], axis=1
    )
    w_less, w_ret, space = to_space(tiles)
    screens[0] = w_less
    screens[1] = w_ret

    def blocks(js):
        acc = [[[None] * 3 for _ in range(4)] for _ in range(2)]
        for kind in range(2):
            for sd in range(16):
                for q in range(3):
                    values = [slab[kind, q, sd, j] for j in js]
                    for a in range(4):
                        factor = sig[kind, q, sd, a]
                        for n in range(2):
                            term = factor * values[n]
                            old = acc[n][a][q]
                            acc[n][a][q] = term if old is None else old + term
        out = []
        for n in range(2):
            re = [acc[n][a][0] - acc[n][a][1] for a in range(4)]
            im = [acc[n][a][2] - acc[n][a][0] - acc[n][a][1] for a in range(4)]
            out.append(re + im)
        return out

    def reduced(r):
        def to_across(piece, carry):
            places = [(z + order(2 * piece + n)) % 8 for n in range(2)]
            out = blocks([(1 - y) * 8 + p for p in places])
            for n in range(2):
                i = 2 * piece + n
                for m in range(8):
                    ysend[r, i, m] = out[n][m]
                push(ysend.at[r, i], yrecv.at[r, i], ys_sem.at[r, i], yr_sem.at[r, i], (across, ka))
            return carry

        lax.fori_loop(0, 4, to_across, 0)

        def mine(piece, carry):
            places = [(z + order(2 * piece + n)) % 8 for n in range(2)]
            out = blocks([y * 8 + p for p in places])
            for n in range(2):
                for m in range(8):
                    own[2 * piece + n, m] = out[n][m]
            return carry

        lax.fori_loop(0, 4, mine, 0)

        for i in range(8):
            arrived(yrecv.at[r, i], yr_sem.at[r, i])
            if i < 7:
                zsend[r, i] = own[i] + yrecv[r, i]
                away = (z + order(i)) % 8
                push(
                    zsend.at[r, i], zrecv.at[r, z], zs_sem.at[r, i], zr_sem.at[r, z],
                    (away * 4 + ta % 4, ka),
                )
        total = own[7] + yrecv[r, 7] + hg[...]
        for i in range(7):
            peer = (z + order(i)) % 8
            arrived(zrecv.at[r, peer], zr_sem.at[r, peer])
            total = total + zrecv[r, peer]
        return total

    for r in range(3):
        if r > 0:
            for d in range(8):
                gsend[r - 1, d] = gbuf[pl.ds(d, 8, stride=8), :]
            exchange(gsend.at[r - 1], grecv.at[r - 1], gs_sem.at[r - 1], gr_sem.at[r - 1])

        rows = [gbuf[8 * m : 8 * m + 8] for m in range(8)]
        for a in range(4):
            re, im = e * rows[a], e * rows[4 + a]
            for b in range(4):
                o_re, o_im = onsite[0, a, b], onsite[1, a, b]
                re = re + o_re * rows[b] - o_im * rows[4 + b]
                im = im + o_re * rows[4 + b] + o_im * rows[b]
            hg[a] = re
            hg[4 + a] = im

        if r > 0:
            collect(grecv.at[r - 1], gr_sem.at[r - 1])
            (space,) = to_space(grecv[r - 1].reshape(64, 128))
        re, im = space[:, :128], space[:, 128:]
        fields = []
        for kind in range(2):
            w_re, w_im = screens[kind, :, :128], screens[kind, :, 128:]
            fields.append(
                jnp.concatenate([-(re * w_im + im * w_re), re * w_re - im * w_im], axis=1)
            )
        sigma = to_momenta(fields)
        for kind in range(2):
            ssend[r, :, kind] = sigma[:, 128 * kind : 128 * kind + 128].reshape(8, 8, 128)
        slot = core * 8 + ka
        for i in range(7, 0, -1):
            peer = (ka + i) % 8
            for n, to in enumerate((ta, sibling)):
                push(
                    ssend.at[r, peer], srecv.at[r, slot], ss_sem.at[r, 2 * i + n],
                    sr_sem.at[r, slot], (to, peer),
                )
        push(
            ssend.at[r, ka], srecv.at[r, slot], ss_sem.at[r, 0], sr_sem.at[r, slot], (sibling, ka)
        )
        srecv[r, slot] = ssend[r, ka]

        if r == 0:
            for kind in range(2):
                for q in range(2):
                    theirs = slab.at[kind, q, pl.ds((1 - core) * 8, 8)]
                    arrived(theirs, or_sem.at[kind, q])
                for d in range(8):
                    sd = (1 - core) * 8 + d
                    slab[kind, 2, sd] = slab[kind, 0, sd] + slab[kind, 1, sd]

        for i in range(8):
            peer = (ka + i) % 8
            for n in range(2):
                if i + n > 0:
                    sd = ((core + n) % 2) * 8 + peer
                    arrived(srecv.at[r, sd], sr_sem.at[r, sd])
        for sd in range(16):
            for kind in range(2):
                tile = srecv[r, sd, kind].astype(BF16).astype(F32)
                for a in range(4):
                    s_re = jnp.broadcast_to(tile[a : a + 1], (8, 128))
                    s_im = jnp.broadcast_to(tile[4 + a : 5 + a], (8, 128))
                    sig[kind, 0, sd, a] = s_re
                    sig[kind, 1, sd, a] = s_im
                    sig[kind, 2, sd, a] = s_re + s_im

        total = reduced(r)
        rate = jnp.concatenate([total[4:], -total[:4]], axis=0).reshape(64, 128)
        if r == 0:
            first[...] = rate
            gbuf[...] = green[...] + time_step * rate
        elif r == 1:
            gbuf[...] = green[...] + (0.5 * time_step) * (first[...] + rate)
        else:
            next_row[...] = green[...] + (0.5 * time_step) * (first[...] + rate)
            derivative[...] = rate

    for i in range(1, 8):
        sent(isend.at[(ka + i) % 8], is_sem.at[i])
    for kind in range(2):
        for q in range(2):
            sent(oslab.at[kind, q], os_sem.at[kind, q])
    for r in range(3):
        for i in range(1, 8):
            if r < 2:
                sent(gsend.at[r, (ka + i) % 8], gs_sem.at[r, i])
            for n in range(2):
                sent(ssend.at[r, (ka + i) % 8], ss_sem.at[r, 2 * i + n])
        sent(ssend.at[r, ka], ss_sem.at[r, 0])
        for i in range(8):
            sent(ysend.at[r, i], ys_sem.at[r, i])
            if i < 7:
                sent(zsend.at[r, i], zs_sem.at[r, i])


def local(
    green_row, screen_lesser, screen_retarded, onsite, lesser_slab, advanced_slab, slab_start,
    block_table,
):
    left, right, twiddle = tables()

    def hbm():
        return pl.BlockSpec(memory_space=pltpu.HBM)

    def vmem():
        return pl.BlockSpec(memory_space=pltpu.VMEM)

    def scratch(*dims, kind=F32):
        return pltpu.VMEM(dims, kind)

    def sems(*dims):
        return pltpu.SemaphoreType.DMA(dims)

    rows = jax.ShapeDtypeStruct((64, 128), F32)
    next_row, derivative = pl.pallas_call(
        kernel,
        name="gw_step",
        out_shape=(rows, rows),
        in_specs=[hbm()] * 11,
        out_specs=(vmem(), vmem()),
        scratch_shapes=[
            pltpu.SMEM((2, 4, 4), F32),
            pltpu.SMEM((32,), jnp.int32),
            pltpu.SMEM((1,), jnp.int32),
            scratch(64, 128),
            scratch(64, 128),
            scratch(64, 128),
            scratch(2, 64, 192, kind=BF16),
            scratch(4, 256, 256, kind=BF16),
            scratch(2, 32, 128),
            scratch(2, 2, 4, 4, 2, 64, 128, kind=BF16),
            scratch(2, 3, 16, 16, 8, 128),
            scratch(2, 2, 8, 16, 8, 128),
            scratch(8, 24, 128),
            scratch(8, 24, 128),
            scratch(2, 8, 8, 128),
            scratch(2, 8, 8, 128),
            scratch(2, 32, 256),
            scratch(3, 8, 2, 8, 128),
            scratch(3, 16, 2, 8, 128),
            scratch(2, 3, 16, 4, 8, 128),
            scratch(8, 8, 8, 128),
            scratch(3, 8, 8, 8, 128),
            scratch(3, 8, 8, 8, 128),
            scratch(3, 7, 8, 8, 128),
            scratch(3, 8, 8, 8, 128),
            scratch(64, 128),
            scratch(8, 8, 128),
            scratch(64, 128),
            sems(11),
            sems(2, 2), sems(2, 2),
            sems(8), sems(8),
            sems(2, 8), sems(2, 8),
            sems(3, 16), sems(3, 16),
            sems(3, 8), sems(3, 8),
            sems(3, 7), sems(3, 8),
        ],
        compiler_params=pltpu.CompilerParams(
            collective_id=0, has_side_effects=True, vmem_limit_bytes=56 * 2**20
        ),
    )(
        onsite,
        block_table,
        slab_start,
        green_row.reshape(64, 128),
        screen_lesser.reshape(64, 128),
        screen_retarded.reshape(64, 128),
        advanced_slab,
        lesser_slab,
        jnp.asarray(left),
        jnp.asarray(right),
        jnp.asarray(twiddle),
    )
    return next_row.reshape(green_row.shape), derivative.reshape(green_row.shape)


def solution(mesh):
    return jax.shard_map(
        local,
        mesh=mesh,
        in_specs=(
            P(None, None, None, "ta", "ka"),
            P(None, None, None, "ta", "ka"),
            P(None, None, None, "ta", "ka"),
            P(),
            P(None, None, None, "ta", None, "ka"),
            P(None, None, None, "ta", None, "ka"),
            P(),
            P(),
        ),
        out_specs=(P(None, None, None, "ta", "ka"), P(None, None, None, "ta", "ka")),
        check_vma=False,
    )
```

time: 94 us -> 83.9 us (0.89)
  local copies, waits for them, and re-layouts: 8.62 us -> 2 us
  Pallas kernels: 83.4 us -> 80.4 us
    unnamed x20 -> x4, local copies, waits for them, and re-layouts: 7.84 us -> 2 us
    pallas_call x1, Pallas kernels: 83.4 us -> 80.4 us  [local(): pl.pallas_call(kernel, name='gw_step', out_shape=(rows, rows), in_specs=[...]
where the time goes in v1:
time: 83.9 us; the launch traced here: 83.7 us
  Pallas kernels  80.4 us (96%)
  local copies, waits for them, and re-layouts  2 us (2%)
  between operations  1.3 us (2%)
    pallas_call x1, Pallas kernels, local(): pl.pallas_call(kernel, name='gw_step', out_shape=(rows, rows), in_specs=[...  80.4 us
    unnamed x4, local copies, waits for them, and re-layouts  2 us

profile of v1, /device:TPU:1, one launch (start us, length us, event | category | flops | bytes accessed | tf_op | source)
XLA Modules:
  0.0 83.7 jit_solution(15171207890981481493)
XLA Ops:
  1.3 80.4 %gw_step.1 = (f32[64,128]{1,0:T(8,128)}, f32[64,128]{1,0:T(8,128)}) custom-call(f32[2,4,4]{2,1,0:T(4,128)} %onsite_hbm.1, s32[32]{0:T(128)} %table_hbm.1, s32[1]{0:T(128)S(6)} %copy.15.begin_hbm, f32[64,128]{1,0:T(8,128)} %bitcast.5, f32[64,128]{1,0:T(8,128)} %bitcast.6, f32[64,128]{1,0:T(8,128)} %bitcast.7, bf16[2,4,4,2,64,128]{5,4,3,2,1,0:T(8,128)(2,1)} %adv_hbm.1, ...), custom_call_target="tpu_custom_call" | custom-call | tf_op jit(solution)/shard_map/gw_step/pallas_call | solution.py:423
  81.7 0.0 copy-start
  81.7 1.4 %copy.16 = f32[2,4,4,2,128]{4,3,2,1,0:T(2,128)} copy(f32[2,4,4,2,128]{4,3,2,1,0:T(2,128)} %bitcast.9) | data formatting | bytes 65536
  83.0 0.0 copy-done
  83.0 0.6 copy.17
Async XLA Ops:
  81.7 1.4 %copy-start = (f32[64,128]{1,0:T(8,128)S(1)}, f32[64,128]{1,0:T(8,128)}, u32[]{:S(2)}) copy-start(f32[64,128]{1,0:T(8,128)} %get-tuple-element.5) | copy-start | bytes 98308

commit v2 on v1

--- a/solution.py
+++ b/solution.py
@@ -92,10 +92,10 @@
     left_hbm, right_hbm, twiddle_hbm,
     next_row, derivative,
     onsite, table, begin, green, less, ret, left, right, twiddle,
-    raw, slab, oslab, isend, irecv, gsend, grecv, screens, ssend, srecv, sig,
-    own, ysend, yrecv, zsend, zrecv, gbuf, hg, first,
+    raw, slab, oslab, isend, irecv, bsend, brecv, screens, ssend, srecv, sig,
+    own, ysend, yrecv, zsend, zrecv, msend, mrecv, orecv, macc, gbuf, hg, first,
     in_sem, os_sem, or_sem, is_sem, ir_sem, gs_sem, gr_sem, ss_sem, sr_sem,
-    ys_sem, yr_sem, zs_sem, zr_sem,
+    ys_sem, yr_sem, zs_sem, zr_sem, ms_sem, mr_sem, oq_sem, ready,
 ):
     ta, ka = lax.axis_index("ta"), lax.axis_index("ka")
     z, y, core = ta // 4, (ta // 2) % 2, ta % 2
@@ -123,6 +123,43 @@
     pl.semaphore_signal(barrier, inc=1, device_id=(sibling, ka), device_id_type=MESH)
     pl.semaphore_signal(barrier, inc=1, device_id=(across, ka), device_id_type=MESH)
 
+    for copy in loads[:4]:
+        copy.wait()
+    for n, ref in enumerate((less, ret, green)):
+        for d in range(8):
+            isend[d, 8 * n : 8 * n + 8, :] = ref[pl.ds(d, 8, stride=8), :]
+    pl.semaphore_wait(barrier, 23)
+
+    def describe(src, dst, ssem, rsem, to):
+        return pltpu.make_async_remote_copy(
+            src_ref=src, dst_ref=dst, send_sem=ssem, recv_sem=rsem,
+            device_id=to, device_id_type=MESH,
+        )
+
+    def push(src, dst, ssem, rsem, to):
+        describe(src, dst, ssem, rsem, to).start()
+
+    def arrived(dst, rsem):
+        describe(dst, dst, rsem, rsem, (sibling, ka)).wait_recv()
+
+    def sent(src, ssem):
+        describe(src, src, ssem, ssem, (sibling, ka)).wait_send()
+
+    def exchange(src, dst, ssem, rsem):
+        for i in range(7, 0, -1):
+            peer = (ka + i) % 8
+            push(src.at[peer], dst.at[ka], ssem.at[i], rsem.at[ka], (ta, peer))
+        dst[ka] = src[ka]
+
+    def collect(dst, rsem):
+        for i in range(1, 8):
+            peer = (ka + i) % 8
+            arrived(dst.at[peer], rsem.at[peer])
+
+    exchange(isend, irecv, is_sem, ir_sem)
+    for i in range(1, 8):
+        pl.semaphore_signal(ready, inc=1, device_id=((ta + 4 * i) % 32, ka), device_id_type=MESH)
+
     row = lax.broadcasted_iota(jnp.int32, (256, 1), 0)
     col = lax.broadcasted_iota(jnp.int32, (256, 256), 1)
     place = row // 8
@@ -132,12 +169,6 @@
     )
     picked = source == col
     lane = lax.broadcasted_iota(jnp.int32, (1, 256), 1) % 64
-    for copy in loads[:4]:
-        copy.wait()
-    for n, ref in enumerate((less, ret, green)):
-        for d in range(8):
-            isend[d, 8 * n : 8 * n + 8, :] = ref[pl.ds(d, 8, stride=8), :]
-    gbuf[...] = green[...]
     tau = jnp.zeros((1, 256), jnp.int32)
     for i in range(32):
         tau = jnp.where(lane // 2 == i, 2 * table[i], tau)
@@ -168,36 +199,6 @@
         return carry
 
     lax.fori_loop(0, 4, relay, 0)
-
-    pl.semaphore_wait(barrier, 23)
-
-    def describe(src, dst, ssem, rsem, to):
-        return pltpu.make_async_remote_copy(
-            src_ref=src, dst_ref=dst, send_sem=ssem, recv_sem=rsem,
-            device_id=to, device_id_type=MESH,
-        )
-
-    def push(src, dst, ssem, rsem, to):
-        describe(src, dst, ssem, rsem, to).start()
-
-    def arrived(dst, rsem):
-        describe(dst, dst, rsem, rsem, (sibling, ka)).wait_recv()
-
-    def sent(src, ssem):
-        describe(src, src, ssem, ssem, (sibling, ka)).wait_send()
-
-    def exchange(src, dst, ssem, rsem):
-        for i in range(7, 0, -1):
-            peer = (ka + i) % 8
-            push(src.at[peer], dst.at[ka], ssem.at[i], rsem.at[ka], (ta, peer))
-        dst[ka] = src[ka]
-
-    def collect(dst, rsem):
-        for i in range(1, 8):
-            peer = (ka + i) % 8
-            arrived(dst.at[peer], rsem.at[peer])
-
-    exchange(isend, irecv, is_sem, ir_sem)
     for kind in range(2):
         for q in range(2):
             push(
@@ -206,14 +207,34 @@
             )
 
     shift = drive_amp * jnp.sin(
-        jnp.full((8, 128), drive_freq, F32) * (begin[0] + 64).astype(F32)
+        jnp.full((64, 128), drive_freq, F32) * (begin[0] + 64).astype(F32)
     )
-    k_lane = lax.broadcasted_iota(jnp.int32, (8, 128), 1)
+    k_lane = lax.broadcasted_iota(jnp.int32, (64, 128), 1)
+    k_row = lax.broadcasted_iota(jnp.int32, (64, 128), 0)
     factor = 2.0 * math.pi / KS
-    e = -2.0 * (
-        jnp.cos((4 * ka + k_lane // KS).astype(F32) * factor + shift)
-        + jnp.cos((k_lane % KS).astype(F32) * factor)
-    )
+
+    def dispersed(group, lane, by):
+        return -2.0 * (
+            jnp.cos((4 * group + lane // KS).astype(F32) * factor + by)
+            + jnp.cos((lane % KS).astype(F32) * factor)
+        )
+
+    e_all = dispersed(k_row // 8, k_lane, shift)
+    e = dispersed(ka, k_lane[:8], shift[:8])
+
+    at_row = lax.broadcasted_iota(jnp.int32, (64, 64), 0)
+    at_col = lax.broadcasted_iota(jnp.int32, (64, 64), 1)
+    entry = jnp.where(at_row // 8 == at_col // 8, at_row % 8 * 8 + at_col % 8, -1)
+    turn = jnp.zeros((64, 64), F32)
+    for a in range(4):
+        for b in range(4):
+            o_re, o_im = onsite[0, a, b], onsite[1, a, b]
+            turn = jnp.where(entry == 8 * a + b, o_re, turn)
+            turn = jnp.where(entry == 8 * (a + 4) + b + 4, o_re, turn)
+            turn = jnp.where(entry == 8 * a + b + 4, -o_im, turn)
+            turn = jnp.where(entry == 8 * (a + 4) + b, o_im, turn)
+    turn_hi, turn_lo = split(turn)
+    turn = jnp.concatenate([turn_hi, turn_lo, turn_hi], axis=1)
 
     tw_c, tw_s = twiddle[0], twiddle[1]
 
@@ -248,17 +269,23 @@
     screens[1] = w_ret
 
     def blocks(js):
-        acc = [[[None] * 3 for _ in range(4)] for _ in range(2)]
-        for kind in range(2):
-            for sd in range(16):
+        def terms(u, acc):
+            kind, half = u // 2, u % 2
+            acc = list(acc)
+            for v in range(8):
+                sd = half * 8 + v
                 for q in range(3):
                     values = [slab[kind, q, sd, j] for j in js]
                     for a in range(4):
                         factor = sig[kind, q, sd, a]
                         for n in range(2):
-                            term = factor * values[n]
-                            old = acc[n][a][q]
-                            acc[n][a][q] = term if old is None else old + term
+                            at = (n * 4 + a) * 3 + q
+                            acc[at] = acc[at] + factor * values[n]
+            return tuple(acc)
+
+        zero = jnp.zeros((8, 128), F32)
+        flat = lax.fori_loop(0, 4, terms, (zero,) * 24)
+        acc = [[flat[(n * 4 + a) * 3 : (n * 4 + a) * 3 + 3] for a in range(4)] for n in range(2)]
         out = []
         for n in range(2):
             re = [acc[n][a][0] - acc[n][a][1] for a in range(4)]
@@ -273,7 +300,7 @@
             for n in range(2):
                 i = 2 * piece + n
                 for m in range(8):
-                    ysend[r, i, m] = out[n][m]
+                    ysend[r, i, 8 * m : 8 * m + 8] = out[n][m]
                 push(ysend.at[r, i], yrecv.at[r, i], ys_sem.at[r, i], yr_sem.at[r, i], (across, ka))
             return carry
 
@@ -284,46 +311,73 @@
             out = blocks([y * 8 + p for p in places])
             for n in range(2):
                 for m in range(8):
-                    own[2 * piece + n, m] = out[n][m]
+                    own[2 * piece + n, 8 * m : 8 * m + 8] = out[n][m]
             return carry
 
         lax.fori_loop(0, 4, mine, 0)
 
+    def to_owner():
         for i in range(8):
-            arrived(yrecv.at[r, i], yr_sem.at[r, i])
+            arrived(yrecv.at[2, i], yr_sem.at[2, i])
             if i < 7:
-                zsend[r, i] = own[i] + yrecv[r, i]
+                zsend[i] = own[i] + yrecv[2, i]
                 away = (z + order(i)) % 8
                 push(
-                    zsend.at[r, i], zrecv.at[r, z], zs_sem.at[r, i], zr_sem.at[r, z],
+                    zsend.at[i], zrecv.at[z], zs_sem.at[i], zr_sem.at[z],
                     (away * 4 + ta % 4, ka),
                 )
-        total = own[7] + yrecv[r, 7] + hg[...]
+        total = own[7] + yrecv[2, 7] + hg[...]
         for i in range(7):
             peer = (z + order(i)) % 8
-            arrived(zrecv.at[r, peer], zr_sem.at[r, peer])
-            total = total + zrecv[r, peer]
+            arrived(zrecv.at[peer], zr_sem.at[peer])
+            total = total + zrecv[peer]
         return total
 
+    def to_fields(r):
+        def tiles_of(i):
+            arrived(yrecv.at[r, i], yr_sem.at[r, i])
+            zsend[i] = own[i] + yrecv[r, i]
+            for d in range(8):
+                msend[r, i, d] = zsend[i, pl.ds(d, 8, stride=8), :]
+
+        def away_block(i, carry):
+            tiles_of(i)
+            away = ((z + order(i)) % 8) * 4 + ta % 4
+            for n in range(8):
+                peer = (ka + 6 + n) % 8
+                push(
+                    msend.at[r, i, peer], mrecv.at[r, z * 8 + ka], ms_sem.at[r, i],
+                    mr_sem.at[r, z], (away, peer),
+                )
+            return carry
+
+        lax.fori_loop(0, 7, away_block, 0)
+        tiles_of(7)
+        for n in range(1, 8):
+            i = (n + 4) % 7 + 1
+            peer = (ka + i) % 8
+            push(
+                msend.at[r, 7, peer], orecv.at[r, i - 1], ms_sem.at[r, 7], oq_sem.at[r],
+                (ta, peer),
+            )
+        total = hg[...]
+        for i in range(7):
+            group = pl.ds(((z + order(i)) % 8) * 8, 8)
+            arrived(mrecv.at[r, group], mr_sem.at[r, (z + order(i)) % 8])
+            total = total + mrecv[r, group].reshape(64, 128)
+        macc[...] = total.reshape(8, 8, 128)
+        macc[ka] += msend[r, 7, ka]
+        arrived(orecv.at[r], oq_sem.at[r])
+        for i in range(1, 8):
+            macc[(ka + 8 - i) % 8] += orecv[r, i - 1]
+        total = macc[...]
+        return jnp.concatenate([total[:, 4:], -total[:, :4]], axis=1).reshape(64, 128)
+
+    green_all = irecv[:, 16:24, :].reshape(64, 128)
+    state = green_all
     for r in range(3):
         if r > 0:
-            for d in range(8):
-                gsend[r - 1, d] = gbuf[pl.ds(d, 8, stride=8), :]
-            exchange(gsend.at[r - 1], grecv.at[r - 1], gs_sem.at[r - 1], gr_sem.at[r - 1])
-
-        rows = [gbuf[8 * m : 8 * m + 8] for m in range(8)]
-        for a in range(4):
-            re, im = e * rows[a], e * rows[4 + a]
-            for b in range(4):
-                o_re, o_im = onsite[0, a, b], onsite[1, a, b]
-                re = re + o_re * rows[b] - o_im * rows[4 + b]
-                im = im + o_re * rows[4 + b] + o_im * rows[b]
-            hg[a] = re
-            hg[4 + a] = im
-
-        if r > 0:
-            collect(grecv.at[r - 1], gr_sem.at[r - 1])
-            (space,) = to_space(grecv[r - 1].reshape(64, 128))
+            (space,) = to_space(state)
         re, im = space[:, :128], space[:, 128:]
         fields = []
         for kind in range(2):
@@ -347,6 +401,14 @@
         )
         srecv[r, slot] = ssend[r, ka]
 
+        if r < 2:
+            hg[...] = left_product(turn, state) + e_all * state
+        else:
+            for d in range(8):
+                bsend[d, :8] = state[8 * d : 8 * d + 8]
+                bsend[d, 8:] = first[8 * d : 8 * d + 8]
+            exchange(bsend, brecv, gs_sem, gr_sem)
+
         if r == 0:
             for kind in range(2):
                 for q in range(2):
@@ -372,33 +434,54 @@
                     sig[kind, 1, sd, a] = s_im
                     sig[kind, 2, sd, a] = s_re + s_im
 
-        total = reduced(r)
-        rate = jnp.concatenate([total[4:], -total[:4]], axis=0).reshape(64, 128)
         if r == 0:
-            first[...] = rate
-            gbuf[...] = green[...] + time_step * rate
-        elif r == 1:
-            gbuf[...] = green[...] + (0.5 * time_step) * (first[...] + rate)
-        else:
-            next_row[...] = green[...] + (0.5 * time_step) * (first[...] + rate)
-            derivative[...] = rate
-
-    for i in range(1, 8):
-        sent(isend.at[(ka + i) % 8], is_sem.at[i])
+            pl.semaphore_wait(ready, 7)
+        reduced(r)
+        if r < 2:
+            rate = to_fields(r)
+            if r == 0:
+                first[...] = rate
+                state = green_all + time_step * rate
+            else:
+                state = green_all + (0.5 * time_step) * (first[...] + rate)
+            continue
+
+        collect(brecv, gr_sem)
+        for d in range(8):
+            gbuf[pl.ds(d, 8, stride=8), :] = brecv[d, :8]
+            first[pl.ds(d, 8, stride=8), :] = brecv[d, 8:]
+        rows = [gbuf[8 * m : 8 * m + 8] for m in range(8)]
+        for a in range(4):
+            re, im = e * rows[a], e * rows[4 + a]
+            for b in range(4):
+                o_re, o_im = onsite[0, a, b], onsite[1, a, b]
+                re = re + o_re * rows[b] - o_im * rows[4 + b]
+                im = im + o_re * rows[4 + b] + o_im * rows[b]
+            hg[8 * a : 8 * a + 8] = re
+            hg[32 + 8 * a : 40 + 8 * a] = im
+        total = to_owner()
+        rate = jnp.concatenate([total[32:], -total[:32]], axis=0)
+        next_row[...] = green[...] + (0.5 * time_step) * (first[...] + rate)
+        derivative[...] = rate
+
     for kind in range(2):
         for q in range(2):
             sent(oslab.at[kind, q], os_sem.at[kind, q])
+    for i in range(1, 8):
+        sent(isend.at[(ka + i) % 8], is_sem.at[i])
+        sent(bsend.at[(ka + i) % 8], gs_sem.at[i])
+        sent(zsend.at[i - 1], zs_sem.at[i - 1])
     for r in range(3):
         for i in range(1, 8):
-            if r < 2:
-                sent(gsend.at[r, (ka + i) % 8], gs_sem.at[r, i])
             for n in range(2):
                 sent(ssend.at[r, (ka + i) % 8], ss_sem.at[r, 2 * i + n])
         sent(ssend.at[r, ka], ss_sem.at[r, 0])
         for i in range(8):
             sent(ysend.at[r, i], ys_sem.at[r, i])
-            if i < 7:
-                sent(zsend.at[r, i], zs_sem.at[r, i])
+        if r < 2:
+            for i in range(7):
+                sent(msend.at[r, i], ms_sem.at[r, i])
+            sent(msend.at[r, 7, pl.ds(0, 7)], ms_sem.at[r, 7])
 
 
 def local(
@@ -441,27 +524,33 @@
             scratch(2, 2, 8, 16, 8, 128),
             scratch(8, 24, 128),
             scratch(8, 24, 128),
-            scratch(2, 8, 8, 128),
-            scratch(2, 8, 8, 128),
+            scratch(8, 16, 128),
+            scratch(8, 16, 128),
             scratch(2, 32, 256),
             scratch(3, 8, 2, 8, 128),
             scratch(3, 16, 2, 8, 128),
             scratch(2, 3, 16, 4, 8, 128),
-            scratch(8, 8, 8, 128),
-            scratch(3, 8, 8, 8, 128),
-            scratch(3, 8, 8, 8, 128),
-            scratch(3, 7, 8, 8, 128),
-            scratch(3, 8, 8, 8, 128),
+            scratch(8, 64, 128),
+            scratch(3, 8, 64, 128),
+            scratch(3, 8, 64, 128),
+            scratch(8, 64, 128),
+            scratch(8, 64, 128),
+            scratch(2, 8, 8, 8, 128),
+            scratch(2, 64, 8, 128),
+            scratch(2, 7, 8, 128),
+            scratch(8, 8, 128),
             scratch(64, 128),
-            scratch(8, 8, 128),
+            scratch(64, 128),
             scratch(64, 128),
             sems(11),
             sems(2, 2), sems(2, 2),
             sems(8), sems(8),
-            sems(2, 8), sems(2, 8),
+            sems(8), sems(8),
             sems(3, 16), sems(3, 16),
             sems(3, 8), sems(3, 8),
-            sems(3, 7), sems(3, 8),
+            sems(7), sems(8),
+            sems(2, 8), sems(2, 8), sems(2),
+            pltpu.SemaphoreType.REGULAR,
         ],
         compiler_params=pltpu.CompilerParams(
             collective_id=0, has_side_effects=True, vmem_limit_bytes=56 * 2**20

time: 83.9 us -> 77.1 us (0.919)
  Pallas kernels: 80.4 us -> 73.7 us
    pallas_call x1, Pallas kernels: 80.4 us -> 73.7 us  [local(): pl.pallas_call(kernel, name='gw_step', out_shape=(rows, rows), in_specs=[...]
where the time goes in v2:
time: 77.1 us; the launch traced here: 76.9 us
  Pallas kernels  73.7 us (96%)
  local copies, waits for them, and re-layouts  2 us (3%)
  between operations  1.3 us (2%)
    pallas_call x1, Pallas kernels, local(): pl.pallas_call(kernel, name='gw_step', out_shape=(rows, rows), in_specs=[...  73.7 us
    unnamed x4, local copies, waits for them, and re-layouts  2 us

profile of v2, /device:TPU:1, one launch (start us, length us, event | category | flops | bytes accessed | tf_op | source)
XLA Modules:
  0.0 76.9 jit_solution(10552010461183450984)
XLA Ops:
  1.3 73.7 %gw_step.1 = (f32[64,128]{1,0:T(8,128)}, f32[64,128]{1,0:T(8,128)}) custom-call(f32[2,4,4]{2,1,0:T(4,128)} %onsite_hbm.1, s32[32]{0:T(128)} %table_hbm.1, s32[1]{0:T(128)S(6)} %copy.15.begin_hbm, f32[64,128]{1,0:T(8,128)} %bitcast.5, f32[64,128]{1,0:T(8,128)} %bitcast.6, f32[64,128]{1,0:T(8,128)} %bitcast.7, bf16[2,4,4,2,64,128]{5,4,3,2,1,0:T(8,128)(2,1)} %adv_hbm.1, ...), custom_call_target="tpu_custom_call" | custom-call | tf_op jit(solution)/shard_map/gw_step/pallas_call | solution.py:506
  74.9 0.0 copy-start
  74.9 1.4 %copy.16 = f32[2,4,4,2,128]{4,3,2,1,0:T(2,128)} copy(f32[2,4,4,2,128]{4,3,2,1,0:T(2,128)} %bitcast.9) | data formatting | bytes 65536
  76.3 0.0 copy-done
  76.3 0.6 copy.17
Async XLA Ops:
  74.9 1.4 %copy-start = (f32[64,128]{1,0:T(8,128)S(1)}, f32[64,128]{1,0:T(8,128)}, u32[]{:S(2)}) copy-start(f32[64,128]{1,0:T(8,128)} %get-tuple-element.5) | copy-start | bytes 98308

commit v3 on v2

--- a/solution.py
+++ b/solution.py
@@ -506,7 +506,7 @@
     next_row, derivative = pl.pallas_call(
         kernel,
         name="gw_step",
-        out_shape=(rows, rows),
+        out_shape=(pltpu.VMEM((64, 128), F32), pltpu.VMEM((64, 128), F32)),
         in_specs=[hbm()] * 11,
         out_specs=(vmem(), vmem()),
         scratch_shapes=[

time: 77.1 us -> 75.6 us (0.981)
    unnamed x4 -> x2, local copies, waits for them, and re-layouts: 2 us -> 1.23 us
where the time goes in v3:
time: 75.6 us; the launch traced here: 75.5 us
  Pallas kernels  73 us (97%)
  between operations  1.29 us (2%)
  local copies, waits for them, and re-layouts  1.23 us (2%)
    pallas_call x1, Pallas kernels, local(): pl.pallas_call(kernel, name='gw_step', out_shape=(pltpu.VMEM((64, 128), F...  73 us

profile of v3, /device:TPU:1, one launch (start us, length us, event | category | flops | bytes accessed | tf_op | source)
XLA Modules:
  0.0 75.5 jit_solution(7615966286714100218)
XLA Ops:
  1.3 73.0 %gw_step.1 = (f32[64,128]{1,0:T(8,128)S(1)}, f32[64,128]{1,0:T(8,128)S(1)}) custom-call(f32[2,4,4]{2,1,0:T(4,128)} %onsite_hbm.1, s32[32]{0:T(128)} %table_hbm.1, s32[1]{0:T(128)S(6)} %copy.17.begin_hbm, f32[64,128]{1,0:T(8,128)} %bitcast.7, f32[64,128]{1,0:T(8,128)} %bitcast.8, f32[64,128]{1,0:T(8,128)} %bitcast.9, bf16[2,4,4,2,64,128]{5,4,3,2,1,0:T(8,128)(2,1)} %adv_hbm.1, ...), custom_call_target="tpu_custom_call" | custom-call | tf_op jit(solution)/shard_map/gw_step/pallas_call | solution.py:506
  74.3 0.6 copy.15
  74.9 0.6 copy.16

commit v4 on v3

--- a/solution.py
+++ b/solution.py
@@ -9,6 +9,7 @@
 from jax.sharding import PartitionSpec as P
 
 KS = 32
+PEERS = ((1, 2), (1, 1), (1, 3), (1, 0), (0, 2), (0, 1), (0, 3), (0, 0))
 MESH = pl.DeviceIdType.MESH
 F32 = jnp.float32
 BF16 = jnp.bfloat16
@@ -101,6 +102,12 @@
     z, y, core = ta // 4, (ta // 2) % 2, ta % 2
     sibling = ta + 1 - 2 * core
     across = ta + 2 - 4 * y
+    x, half = ka % 4, ka // 4
+
+    def peer_of(n, sign=1):
+        to_half, to_x = PEERS[n]
+        return (half + to_half) % 2 * 4 + (x + 4 + sign * to_x) % 4
+
 
     loads = [
         pltpu.make_async_copy(src, dst, in_sem.at[i])
@@ -146,9 +153,9 @@
         describe(src, src, ssem, ssem, (sibling, ka)).wait_send()
 
     def exchange(src, dst, ssem, rsem):
-        for i in range(7, 0, -1):
-            peer = (ka + i) % 8
-            push(src.at[peer], dst.at[ka], ssem.at[i], rsem.at[ka], (ta, peer))
+        for n in range(7):
+            peer = peer_of(n)
+            push(src.at[peer], dst.at[ka], ssem.at[n], rsem.at[ka], (ta, peer))
         dst[ka] = src[ka]
 
     def collect(dst, rsem):
@@ -344,7 +351,7 @@
             tiles_of(i)
             away = ((z + order(i)) % 8) * 4 + ta % 4
             for n in range(8):
-                peer = (ka + 6 + n) % 8
+                peer = peer_of(n)
                 push(
                     msend.at[r, i, peer], mrecv.at[r, z * 8 + ka], ms_sem.at[r, i],
                     mr_sem.at[r, z], (away, peer),
@@ -353,12 +360,10 @@
 
         lax.fori_loop(0, 7, away_block, 0)
         tiles_of(7)
-        for n in range(1, 8):
-            i = (n + 4) % 7 + 1
-            peer = (ka + i) % 8
+        for n in range(7):
+            peer = peer_of(n)
             push(
-                msend.at[r, 7, peer], orecv.at[r, i - 1], ms_sem.at[r, 7], oq_sem.at[r],
-                (ta, peer),
+                msend.at[r, 7, peer], orecv.at[r, n], ms_sem.at[r, 7], oq_sem.at[r], (ta, peer)
             )
         total = hg[...]
         for i in range(7):
@@ -368,8 +373,8 @@
         macc[...] = total.reshape(8, 8, 128)
         macc[ka] += msend[r, 7, ka]
         arrived(orecv.at[r], oq_sem.at[r])
-        for i in range(1, 8):
-            macc[(ka + 8 - i) % 8] += orecv[r, i - 1]
+        for n in range(7):
+            macc[peer_of(n, -1)] += orecv[r, n]
         total = macc[...]
         return jnp.concatenate([total[:, 4:], -total[:, :4]], axis=1).reshape(64, 128)
 
@@ -389,15 +394,15 @@
         for kind in range(2):
             ssend[r, :, kind] = sigma[:, 128 * kind : 128 * kind + 128].reshape(8, 8, 128)
         slot = core * 8 + ka
-        for i in range(7, 0, -1):
-            peer = (ka + i) % 8
-            for n, to in enumerate((ta, sibling)):
+        for i in range(7):
+            peer = peer_of(i)
+            for n, to in enumerate((sibling, ta)):
                 push(
                     ssend.at[r, peer], srecv.at[r, slot], ss_sem.at[r, 2 * i + n],
                     sr_sem.at[r, slot], (to, peer),
                 )
         push(
-            ssend.at[r, ka], srecv.at[r, slot], ss_sem.at[r, 0], sr_sem.at[r, slot], (sibling, ka)
+            ssend.at[r, ka], srecv.at[r, slot], ss_sem.at[r, 14], sr_sem.at[r, slot], (sibling, ka)
         )
         srecv[r, slot] = ssend[r, ka]
 
@@ -467,15 +472,15 @@
     for kind in range(2):
         for q in range(2):
             sent(oslab.at[kind, q], os_sem.at[kind, q])
-    for i in range(1, 8):
-        sent(isend.at[(ka + i) % 8], is_sem.at[i])
-        sent(bsend.at[(ka + i) % 8], gs_sem.at[i])
-        sent(zsend.at[i - 1], zs_sem.at[i - 1])
+    for n in range(7):
+        sent(isend.at[peer_of(n)], is_sem.at[n])
+        sent(bsend.at[peer_of(n)], gs_sem.at[n])
+        sent(zsend.at[n], zs_sem.at[n])
     for r in range(3):
-        for i in range(1, 8):
+        for i in range(7):
             for n in range(2):
-                sent(ssend.at[r, (ka + i) % 8], ss_sem.at[r, 2 * i + n])
-        sent(ssend.at[r, ka], ss_sem.at[r, 0])
+                sent(ssend.at[r, peer_of(i)], ss_sem.at[r, 2 * i + n])
+        sent(ssend.at[r, ka], ss_sem.at[r, 14])
         for i in range(8):
             sent(ysend.at[r, i], ys_sem.at[r, i])
         if r < 2:

time: 75.6 us -> 73.8 us (0.976)
  Pallas kernels: 73 us -> 71.2 us
    pallas_call x1, Pallas kernels: 73 us -> 71.2 us  [local(): pl.pallas_call(kernel, name='gw_step', out_shape=(pltpu.VMEM((64, 128), F...]
where the time goes in v4:
time: 73.8 us; the launch traced here: 73.7 us
  Pallas kernels  71.2 us (96%)
  between operations  1.29 us (2%)
  local copies, waits for them, and re-layouts  1.23 us (2%)
    pallas_call x1, Pallas kernels, local(): pl.pallas_call(kernel, name='gw_step', out_shape=(pltpu.VMEM((64, 128), F...  71.2 us

profile of v4, /device:TPU:1, one launch (start us, length us, event | category | flops | bytes accessed | tf_op | source)
XLA Modules:
  0.0 73.7 jit_solution(2059577696481742719)
XLA Ops:
  1.3 71.2 %gw_step.1 = (f32[64,128]{1,0:T(8,128)S(1)}, f32[64,128]{1,0:T(8,128)S(1)}) custom-call(f32[2,4,4]{2,1,0:T(4,128)} %onsite_hbm.1, s32[32]{0:T(128)} %table_hbm.1, s32[1]{0:T(128)S(6)} %copy.17.begin_hbm, f32[64,128]{1,0:T(8,128)} %bitcast.7, f32[64,128]{1,0:T(8,128)} %bitcast.8, f32[64,128]{1,0:T(8,128)} %bitcast.9, bf16[2,4,4,2,64,128]{5,4,3,2,1,0:T(8,128)(2,1)} %adv_hbm.1, ...), custom_call_target="tpu_custom_call" | custom-call | tf_op jit(solution)/shard_map/gw_step/pallas_call | solution.py:511
  72.4 0.6 copy.15
  73.1 0.6 copy.16

commit v5 on v4

--- a/solution.py
+++ b/solution.py
@@ -109,6 +109,15 @@
         return (half + to_half) % 2 * 4 + (x + 4 + sign * to_x) % 4
 
 
+    barrier = pltpu.get_barrier_semaphore()
+    for n in range(7):
+        for to in (
+            (ta, peer_of(n)), (sibling, peer_of(n)), ((z + order(n)) % 8 * 4 + ta % 4, ka)
+        ):
+            pl.semaphore_signal(barrier, inc=1, device_id=to, device_id_type=MESH)
+    pl.semaphore_signal(barrier, inc=1, device_id=(across, ka), device_id_type=MESH)
+    pl.semaphore_signal(barrier, inc=1, device_id=(sibling, ka), device_id_type=MESH)
+
     loads = [
         pltpu.make_async_copy(src, dst, in_sem.at[i])
         for i, (src, dst) in enumerate(
@@ -121,14 +130,6 @@
     ]
     for copy in loads:
         copy.start()
-
-    barrier = pltpu.get_barrier_semaphore()
-    for i in range(1, 8):
-        pl.semaphore_signal(barrier, inc=1, device_id=(ta, (ka + i) % 8), device_id_type=MESH)
-        pl.semaphore_signal(barrier, inc=1, device_id=(sibling, (ka + i) % 8), device_id_type=MESH)
-        pl.semaphore_signal(barrier, inc=1, device_id=((ta + 4 * i) % 32, ka), device_id_type=MESH)
-    pl.semaphore_signal(barrier, inc=1, device_id=(sibling, ka), device_id_type=MESH)
-    pl.semaphore_signal(barrier, inc=1, device_id=(across, ka), device_id_type=MESH)
 
     for copy in loads[:4]:
         copy.wait()
@@ -333,6 +334,19 @@
                     zsend.at[i], zrecv.at[z], zs_sem.at[i], zr_sem.at[z],
                     (away * 4 + ta % 4, ka),
                 )
+        collect(brecv, gr_sem)
+        for d in range(8):
+            gbuf[pl.ds(d, 8, stride=8), :] = brecv[d, :8]
+            first[pl.ds(d, 8, stride=8), :] = brecv[d, 8:]
+        rows = [gbuf[8 * m : 8 * m + 8] for m in range(8)]
+        for a in range(4):
+            re, im = e * rows[a], e * rows[4 + a]
+            for b in range(4):
+                o_re, o_im = onsite[0, a, b], onsite[1, a, b]
+                re = re + o_re * rows[b] - o_im * rows[4 + b]
+                im = im + o_re * rows[4 + b] + o_im * rows[b]
+            hg[8 * a : 8 * a + 8] = re
+            hg[32 + 8 * a : 40 + 8 * a] = im
         total = own[7] + yrecv[2, 7] + hg[...]
         for i in range(7):
             peer = (z + order(i)) % 8
@@ -394,9 +408,9 @@
         for kind in range(2):
             ssend[r, :, kind] = sigma[:, 128 * kind : 128 * kind + 128].reshape(8, 8, 128)
         slot = core * 8 + ka
-        for i in range(7):
-            peer = peer_of(i)
-            for n, to in enumerate((sibling, ta)):
+        for n, to in enumerate((sibling, ta)):
+            for i in range(7):
+                peer = peer_of(i)
                 push(
                     ssend.at[r, peer], srecv.at[r, slot], ss_sem.at[r, 2 * i + n],
                     sr_sem.at[r, slot], (to, peer),
@@ -423,21 +437,19 @@
                     sd = (1 - core) * 8 + d
                     slab[kind, 2, sd] = slab[kind, 0, sd] + slab[kind, 1, sd]
 
-        for i in range(8):
-            peer = (ka + i) % 8
+        for i in range(7, -1, -1):
             for n in range(2):
-                if i + n > 0:
-                    sd = ((core + n) % 2) * 8 + peer
+                sd = ((core + n) % 2) * 8 + peer_of(i)
+                if i < 7 or n > 0:
                     arrived(srecv.at[r, sd], sr_sem.at[r, sd])
-        for sd in range(16):
-            for kind in range(2):
-                tile = srecv[r, sd, kind].astype(BF16).astype(F32)
-                for a in range(4):
-                    s_re = jnp.broadcast_to(tile[a : a + 1], (8, 128))
-                    s_im = jnp.broadcast_to(tile[4 + a : 5 + a], (8, 128))
-                    sig[kind, 0, sd, a] = s_re
-                    sig[kind, 1, sd, a] = s_im
-                    sig[kind, 2, sd, a] = s_re + s_im
+                for kind in range(2):
+                    tile = srecv[r, sd, kind].astype(BF16).astype(F32)
+                    for a in range(4):
+                        s_re = jnp.broadcast_to(tile[a : a + 1], (8, 128))
+                        s_im = jnp.broadcast_to(tile[4 + a : 5 + a], (8, 128))
+                        sig[kind, 0, sd, a] = s_re
+                        sig[kind, 1, sd, a] = s_im
+                        sig[kind, 2, sd, a] = s_re + s_im
 
         if r == 0:
             pl.semaphore_wait(ready, 7)
@@ -451,19 +463,6 @@
                 state = green_all + (0.5 * time_step) * (first[...] + rate)
             continue
 
-        collect(brecv, gr_sem)
-        for d in range(8):
-            gbuf[pl.ds(d, 8, stride=8), :] = brecv[d, :8]
-            first[pl.ds(d, 8, stride=8), :] = brecv[d, 8:]
-        rows = [gbuf[8 * m : 8 * m + 8] for m in range(8)]
-        for a in range(4):
-            re, im = e * rows[a], e * rows[4 + a]
-            for b in range(4):
-                o_re, o_im = onsite[0, a, b], onsite[1, a, b]
-                re = re + o_re * rows[b] - o_im * rows[4 + b]
-                im = im + o_re * rows[4 + b] + o_im * rows[b]
-            hg[8 * a : 8 * a + 8] = re
-            hg[32 + 8 * a : 40 + 8 * a] = im
         total = to_owner()
         rate = jnp.concatenate([total[32:], -total[:32]], axis=0)
         next_row[...] = green[...] + (0.5 * time_step) * (first[...] + rate)

time: 73.8 us -> 73.5 us (level)
  Pallas kernels: 71.2 us -> 70.2 us
    pallas_call x1, Pallas kernels: 71.2 us -> 70.2 us  [local(): pl.pallas_call(kernel, name='gw_step', out_shape=(pltpu.VMEM((64, 128), F...]
where the time goes in v5:
time: 73.5 us; the launch traced here: 72.8 us
  Pallas kernels  70.2 us (96%)
  between operations  1.29 us (2%)
  local copies, waits for them, and re-layouts  1.23 us (2%)
    pallas_call x1, Pallas kernels, local(): pl.pallas_call(kernel, name='gw_step', out_shape=(pltpu.VMEM((64, 128), F...  70.2 us

profile of v5, /device:TPU:1, one launch (start us, length us, event | category | flops | bytes accessed | tf_op | source)
XLA Modules:
  0.0 72.8 jit_solution(16524512963598821159)
XLA Ops:
  1.3 70.2 %gw_step.1 = (f32[64,128]{1,0:T(8,128)S(1)}, f32[64,128]{1,0:T(8,128)S(1)}) custom-call(f32[2,4,4]{2,1,0:T(4,128)} %onsite_hbm.1, s32[32]{0:T(128)} %table_hbm.1, s32[1]{0:T(128)S(6)} %copy.17.begin_hbm, f32[64,128]{1,0:T(8,128)} %bitcast.7, f32[64,128]{1,0:T(8,128)} %bitcast.8, f32[64,128]{1,0:T(8,128)} %bitcast.9, bf16[2,4,4,2,64,128]{5,4,3,2,1,0:T(8,128)(2,1)} %adv_hbm.1, ...), custom_call_target="tpu_custom_call" | custom-call | tf_op jit(solution)/shard_map/gw_step/pallas_call | solution.py:510
  71.5 0.6 copy.15
  72.2 0.6 copy.16

commit v6 on v5

--- a/solution.py
+++ b/solution.py
@@ -277,11 +277,9 @@
     screens[1] = w_ret
 
     def blocks(js):
-        def terms(u, acc):
-            kind, half = u // 2, u % 2
+        def terms(kind, acc):
             acc = list(acc)
-            for v in range(8):
-                sd = half * 8 + v
+            for sd in range(16):
                 for q in range(3):
                     values = [slab[kind, q, sd, j] for j in js]
                     for a in range(4):
@@ -292,7 +290,7 @@
             return tuple(acc)
 
         zero = jnp.zeros((8, 128), F32)
-        flat = lax.fori_loop(0, 4, terms, (zero,) * 24)
+        flat = lax.fori_loop(0, 2, terms, (zero,) * 24)
         acc = [[flat[(n * 4 + a) * 3 : (n * 4 + a) * 3 + 3] for a in range(4)] for n in range(2)]
         out = []
         for n in range(2):
@@ -309,7 +307,12 @@
                 i = 2 * piece + n
                 for m in range(8):
                     ysend[r, i, 8 * m : 8 * m + 8] = out[n][m]
-                push(ysend.at[r, i], yrecv.at[r, i], ys_sem.at[r, i], yr_sem.at[r, i], (across, ka))
+                for part in range(2):
+                    rows = pl.ds(32 * part, 32)
+                    push(
+                        ysend.at[r, i, rows], yrecv.at[r, i, rows], ys_sem.at[r, i],
+                        yr_sem.at[r, i], (across, ka),
+                    )
             return carry
 
         lax.fori_loop(0, 4, to_across, 0)

time: 73.5 us -> 73.3 us (level)
  no operation moved by 1% of the time
where the time goes in v6:
time: 73.3 us; the launch traced here: 73.2 us
  Pallas kernels  70.7 us (96%)
  between operations  1.29 us (2%)
  local copies, waits for them, and re-layouts  1.23 us (2%)
    pallas_call x1, Pallas kernels, local(): pl.pallas_call(kernel, name='gw_step', out_shape=(pltpu.VMEM((64, 128), F...  70.7 us

profile of v6, /device:TPU:1, one launch (start us, length us, event | category | flops | bytes accessed | tf_op | source)
XLA Modules:
  0.0 73.2 jit_solution(12867201352743403263)
XLA Ops:
  1.3 70.7 %gw_step.1 = (f32[64,128]{1,0:T(8,128)S(1)}, f32[64,128]{1,0:T(8,128)S(1)}) custom-call(f32[2,4,4]{2,1,0:T(4,128)} %onsite_hbm.1, s32[32]{0:T(128)} %table_hbm.1, s32[1]{0:T(128)S(6)} %copy.17.begin_hbm, f32[64,128]{1,0:T(8,128)} %bitcast.7, f32[64,128]{1,0:T(8,128)} %bitcast.8, f32[64,128]{1,0:T(8,128)} %bitcast.9, bf16[2,4,4,2,64,128]{5,4,3,2,1,0:T(8,128)(2,1)} %adv_hbm.1, ...), custom_call_target="tpu_custom_call" | custom-call | tf_op jit(solution)/shard_map/gw_step/pallas_call | solution.py:513
  72.0 0.6 copy.15
  72.6 0.6 copy.16
